TPU v7x, 256 devices: a whole 4x4x8 slice. The times are simulated.
256 devices in a mesh: row: 16 (over z, y_hi), col: 16 (over x, y_lo, core).
Axes of the slice: x: 4, y: 4 (y_hi: 2, y_lo: 2; y = y_hi * 2 + y_lo), z: 8, core: 2. Of those that a mesh axis runs over, the one named last changes fastest.
Arguments:
- amplitudes: float32 [16, 16, 400, 400], P('row', None, 'col'), may hold values from -6 to 6
- integrals: float32 [64, 64, 400, 400], P('row', None, 'col'), may hold values from -0.015625 to 0.015625
- rest: float32 [16, 16, 64, 64], P('col', None, 'row'), may hold values from -6 to 6
- occ_energy: float32 [16], replicated, may hold values from -2 to -0.5
- vir_energy: float32 [64], replicated, may hold values from 0.5 to 3
Outputs:
- new_amps: float32 [16, 16, 64, 64], P('col', None, 'row')
All inputs are finite; a program needn't handle non-finite values.
Results may differ from a plain program's by a relative error of at most 0.000057.
Values sent between devices are 32-bit elements; how exact they have to be, the bound alone decides.
No kernel may reach another device: no remote copies, remote signals or barrier semaphores. Data moves between devices by JAX's collectives and lax.ppermute only.
A program may use at most 128 MiB of HBM per device.

v0:
```python
import jax
import jax.numpy as jnp
from jax import lax
from jax.sharding import PartitionSpec as P


def on_device(amplitudes, integrals, rest, occ_energy, vir_energy):
    row_index = lax.axis_index("row")
    col_index = lax.axis_index("col")
    a_count = integrals.shape[0]
    b_count = integrals.shape[1]
    integral_slab = integrals.reshape(a_count * b_count, -1)
    occupied = amplitudes.shape[1]
    shard_piece = lax.all_gather(amplitudes, "row", axis=0, tiled=True)
    piece_rows = shard_piece.shape[0]
    flattened = shard_piece.reshape(piece_rows * occupied, -1)
    product = lax.dot_general(
        flattened,
        integral_slab,
        (((1,), (1,)), ((), ())),
        precision=lax.Precision.HIGHEST,
        preferred_element_type=jnp.float32,
    )
    partial_value = product.reshape(piece_rows, occupied, a_count, b_count)
    summed = lax.psum_scatter(partial_value, "col", scatter_dimension=0, tiled=True)
    moved = lax.all_to_all(
        lax.all_to_all(summed, "row", split_axis=3, concat_axis=2, tiled=True),
        "col",
        split_axis=1,
        concat_axis=0,
        tiled=True,
    )
    combined = summed + jnp.transpose(moved, (1, 0, 3, 2))
    i_count = combined.shape[0]
    occ_local = lax.dynamic_slice_in_dim(occ_energy, col_index * i_count, i_count, 0)
    vir_local = lax.dynamic_slice_in_dim(vir_energy, row_index * a_count, a_count, 0)
    denominator = (
        vir_local[None, None, :, None]
        + vir_energy[None, None, None, :]
        - occ_local[:, None, None, None]
        - occ_energy[None, :, None, None]
    )
    return (combined + rest) / denominator


def solution(mesh):
    in_specs = (
        P("row", None, "col", None),
        P("row", None, "col", None),
        P("col", None, "row", None),
        P(),
        P(),
    )
    out_specs = P("col", None, "row", None)
    return jax.shard_map(
        on_device, mesh=mesh, in_specs=in_specs, out_specs=out_specs, check_vma=False
    )
```

profile of v0, /device:TPU:1, one launch (start us, length us, event | category | flops | bytes accessed | tf_op | source)
XLA Modules:
  0.0 327.3 jit_solution(11584524614010061250)
XLA Ops:
  6.5 0.7 all-gather.2.cloned.1.call-update
  7.3 0.0 reduce-scatter.2.cloned.1.call-start
  7.3 189.7 %all-gather.2.cloned.1.call-done = f32[16,16,25,400]{3,1,2,0:T(8,128)} async-done(((f32[1,16,25,400]{3,1,2,0:T(8,128)}), f32[16,16,25,400]{3,1,2,0:T(8,128)}) %all-gather.2.cloned.1.call-update) | async-done | bytes 10240016 | tf_op jit(solution)/shard_map/all_gather | solution.py:14
  197.0 26.4 %fusion.3 = f32[16,16,4,64]{3,1,2,0:T(8,128)} fusion(f32[4,64,25,400]{3,1,2,0:T(8,128)} %param.6, f32[16,16,25,400]{3,1,2,0:T(8,128)} %all-gather.2.cloned.1.call-done), kind=kOutput, calls=%fused_computation.3 | convolution fusion | flops 7864320000 | bytes 20742144 | tf_op jit(solution)/shard_map/dot_general | solution.py:17
  223.4 58.5 %reduce-scatter.2.cloned.1.call-done = f32[1,16,4,64]{3,1,2,0:T(8,128)} async-done(((f32[16,16,4,64]{3,1,2,0:T(8,128)}), f32[1,16,4,64]{3,1,2,0:T(8,128)}) %reduce-scatter.2.cloned.1.call-update) | async-done | bytes 16400 | tf_op jit(solution)/shard_map/reduce_scatter | solution.py:25
  281.9 0.9 copy.14
  282.8 0.7 reshape.59
  283.5 9.0 %all-to-all-start = ((f32[16,1,256]{2,1,0:T(1,128)}), f32[16,1,256]{2,1,0:T(1,128)S(1)}, u32[]{:S(2)}, u32[]{:S(2)}) async-start(f32[16,1,256]{2,1,0:T(1,128)} %reshape.59), calls=%async_computation.1 | async-start | bytes 32768 | tf_op jit(solution)/shard_map/all_to_all | solution.py:27
  292.6 0.6 dynamic_slice.7
  293.2 0.1 dynamic_slice.6
  293.2 8.2 %all-to-all-done = f32[16,1,256]{2,1,0:T(1,128)S(1)} async-done(((f32[16,1,256]{2,1,0:T(1,128)}), f32[16,1,256]{2,1,0:T(1,128)S(1)}, u32[]{:S(2)}, u32[]{:S(2)}) %all-to-all-start) | async-done | bytes 16416 | tf_op jit(solution)/shard_map/all_to_all | solution.py:27
  301.5 0.6 broadcast.48
  302.1 0.7 reduce
  302.8 0.1 reshape.60
  303.0 0.1 copy.16
  303.1 0.1 copy.17
  303.2 0.7 reshape.61
  303.9 8.4 %all-to-all-start.1 = ((f32[16,1,256]{2,1,0:T(1,128)}), f32[16,1,256]{2,1,0:T(1,128)S(1)}, u32[]{:S(2)}, u32[]{:S(2)}) async-start(f32[16,1,256]{2,1,0:T(1,128)} %reshape.61), calls=%async_computation.2 | async-start | bytes 32768 | tf_op jit(solution)/shard_map/all_to_all | solution.py:26
  312.3 0.6 add_subtract_fusion
  312.9 5.2 %all-to-all-done.1 = f32[16,1,256]{2,1,0:T(1,128)S(1)} async-done(((f32[16,1,256]{2,1,0:T(1,128)}), f32[16,1,256]{2,1,0:T(1,128)S(1)}, u32[]{:S(2)}, u32[]{:S(2)}) %all-to-all-start.1) | async-done | bytes 16416 | tf_op jit(solution)/shard_map/all_to_all | solution.py:26
  318.2 0.7 reduce.1
  318.9 0.1 reshape.62
  319.0 0.8 fusion.9
  319.8 0.6 copy.20
  (9 shorter events, 0.0 us)
Async XLA Ops:
  6.5 190.5 %all-gather.2.cloned.1.call-start = ((), (), s32[]{:S(2)}) async-start(), calls=%async_computation.3 | async-start | bytes 13926400 | tf_op jit(solution)/shard_map/all_gather | solution.py:14
  7.3 285.3 %copy-start.1 = (f32[16]{0:T(128)S(1)}, f32[16]{0:T(128)}, u32[]{:S(2)}) copy-start(f32[16]{0:T(128)} %param.8) | copy-start | bytes 196
  7.3 285.9 %copy-start.2 = (f32[64]{0:T(128)S(1)}, f32[64]{0:T(128)}, u32[]{:S(2)}) copy-start(f32[64]{0:T(128)} %param.9) | copy-start | bytes 772
  7.3 311.7 %copy-start = (f32[1,16,4,64]{3,2,1,0:T(4,128)S(1)}, f32[1,16,4,64]{3,2,1,0:T(4,128)}, u32[]{:S(2)}) copy-start(f32[1,16,4,64]{3,2,1,0:T(4,128)} %param.7) | copy-start | bytes 49156
  7.3 274.6 %reduce-scatter.2.cloned.1.call-start = ((), (), s32[]{:S(2)}) async-start(), calls=%async_computation.4 | async-start | bytes 557056 | tf_op jit(solution)/shard_map/reduce_scatter | solution.py:25
  283.5 18.0 %all-to-all-start = ((f32[16,1,256]{2,1,0:T(1,128)}), f32[16,1,256]{2,1,0:T(1,128)S(1)}, u32[]{:S(2)}, u32[]{:S(2)}) async-start(f32[16,1,256]{2,1,0:T(1,128)} %reshape.59), calls=%async_computation.1 | async-start | bytes 32768 | tf_op jit(solution)/shard_map/all_to_all | solution.py:27
  303.9 14.3 %all-to-all-start.1 = ((f32[16,1,256]{2,1,0:T(1,128)}), f32[16,1,256]{2,1,0:T(1,128)S(1)}, u32[]{:S(2)}, u32[]{:S(2)}) async-start(f32[16,1,256]{2,1,0:T(1,128)} %reshape.61), calls=%async_computation.2 | async-start | bytes 32768 | tf_op jit(solution)/shard_map/all_to_all | solution.py:26
Sparse Core Ops, SparseCore 0:
  9.9 187.0 all-gather.1
  223.5 58.3 reduce-scatter.1
where the time goes:
time: 328 us; the launch traced here: 327 us
  waiting for transfers between devices  262 us (80%)
  matrix products  26.4 us (8%)
  starting transfers between devices  17.5 us (5%)
  between operations  13.5 us (4%)
  local copies, waits for them, and re-layouts  4.61 us (1%)
    all_gather x1, waiting for transfers between devices, on_device(): shard_piece = lax.all_gather(amplitudes, 'row', axis=0, tiled=True)  190 us
    reduce_scatter x1, waiting for transfers between devices, on_device(): lax.psum_scatter(partial_value, 'col', scatter_dimension=0, tiled=True)  58.5 us
    dot_general x1, matrix products, on_device(): lax.dot_general(flattened, integral_slab, (((1,), (1,)), ((), ())), preci...  26.4 us
    all_to_all x1, starting transfers between devices, on_device(): lax.all_to_all(summed, 'row', split_axis=3, concat_axis=2, tiled=True)  9.03 us
    all_to_all x1, starting transfers between devices, on_device(): lax.all_to_all(lax.all_to_all(summed, 'row', split_axis=3, concat_axis=2,...  8.43 us
    all_to_all x1, waiting for transfers between devices, on_device(): lax.all_to_all(summed, 'row', split_axis=3, concat_axis=2, tiled=True)  8.25 us
  transfers between devices with their start and end apart: 4, of which 4 were waited for; matrix products, arithmetic and copies ran while one was open for 0% of the time, Pallas kernels for 0%

commit v1 on v0

--- a/solution.py
+++ b/solution.py
@@ -11,7 +11,9 @@
     b_count = integrals.shape[1]
     integral_slab = integrals.reshape(a_count * b_count, -1)
     occupied = amplitudes.shape[1]
-    shard_piece = lax.all_gather(amplitudes, "row", axis=0, tiled=True)
+    shard_piece = jnp.concatenate(
+        lax.all_to_all(jnp.stack([amplitudes] * lax.axis_size("row")), "row", 0, 0), axis=0
+    )
     piece_rows = shard_piece.shape[0]
     flattened = shard_piece.reshape(piece_rows * occupied, -1)
     product = lax.dot_general(

time: 328 us -> 486 us (1.48)
  local copies, waits for them, and re-layouts: 4.61 us -> 83.5 us
  waiting for transfers between devices: 262 us -> 336 us
  starting transfers between devices: 17.5 us -> 29.3 us
  matrix products: 26.4 us -> 20.9 us
    all_to_all x0 -> x1, waiting for transfers between devices: none -> 261 us  [on_device(): lax.all_to_all(jnp.stack([amplitudes] * lax.axis_size('row')), 'row', 0, 0)]
    all_gather x1 -> x0, waiting for transfers between devices: 190 us -> none  [on_device(): shard_piece = lax.all_gather(amplitudes, 'row', axis=0, tiled=True)]
    dot_general x0 -> x2, local copies, waits for them, and re-layouts: none -> 31.7 us  [on_device(): lax.dot_general(flattened, integral_slab, (((1,), (1,)), ((), ())), preci...]
    all_to_all x0 -> x1, local copies, waits for them, and re-layouts: none -> 21.4 us  [on_device(): lax.all_to_all(jnp.stack([amplitudes] * lax.axis_size('row')), 'row', 0, 0)]
    unnamed x10 -> x11, local copies, waits for them, and re-layouts: 1.69 us -> 20 us
    all_to_all x0 -> x1, starting transfers between devices: none -> 11.8 us  [on_device(): lax.all_to_all(jnp.stack([amplitudes] * lax.axis_size('row')), 'row', 0, 0)]
    another operation x0 -> x1, local copies, waits for them, and re-layouts: none -> 7.51 us  [on_device(): jnp.stack([amplitudes] * lax.axis_size('row'))]
    dot_general x1, matrix products: 26.4 us -> 20.9 us  [on_device(): lax.dot_general(flattened, integral_slab, (((1,), (1,)), ((), ())), preci...]
  transfers between devices with their start and end apart: 4 -> 4, of which waited for: 4 -> 4; matrix products, arithmetic and copies ran while one was open for 0% -> 7% of each run, Pallas kernels for 0% -> 0%
where the time goes in v1:
time: 486 us
  waiting for transfers between devices  336 us (69%)
  local copies, waits for them, and re-layouts  83.5 us (17%)
  starting transfers between devices  29.3 us (6%)
  matrix products  20.9 us (4%)
  between operations  13.5 us (3%)
    all_to_all x1, waiting for transfers between devices, on_device(): lax.all_to_all(jnp.stack([amplitudes] * lax.axis_size('row')), 'row', 0, 0)  261 us
    reduce_scatter x1, waiting for transfers between devices, on_device(): lax.psum_scatter(partial_value, 'col', scatter_dimension=0, tiled=True)  61 us
    dot_general x2, local copies, waits for them, and re-layouts, on_device(): lax.dot_general(flattened, integral_slab, (((1,), (1,)), ((), ())), preci...  31.7 us
    all_to_all x1, local copies, waits for them, and re-layouts, on_device(): lax.all_to_all(jnp.stack([amplitudes] * lax.axis_size('row')), 'row', 0, 0)  21.4 us
    dot_general x1, matrix products, on_device(): lax.dot_general(flattened, integral_slab, (((1,), (1,)), ((), ())), preci...  20.9 us
    unnamed x11, local copies, waits for them, and re-layouts  20 us
    all_to_all x1, starting transfers between devices, on_device(): lax.all_to_all(jnp.stack([amplitudes] * lax.axis_size('row')), 'row', 0, 0)  11.8 us
  transfers between devices with their start and end apart: 4, of which 4 were waited for; matrix products, arithmetic and copies ran while one was open for 7% of the time, Pallas kernels for 0%

profile of v1, /device:TPU:1, one launch (start us, length us, event | category | flops | bytes accessed | tf_op | source)
XLA Modules:
  0.0 485.6 jit_solution(8617481606993832290)
XLA Ops:
  6.5 7.5 %stack.2 = f32[16,1,16,25,400]{4,2,3,1,0:T(8,128)} broadcast(f32[16,25,400]{2,0,1:T(8,128)} %bitcast.24), dimensions={2,3,4} | broadcast | bytes 10880000 | tf_op jit(solution)/shard_map/stack | solution.py:15
  14.0 11.8 %all-to-all-start = ((f32[16,1,16,25,400]{4,2,3,1,0:T(8,128)}), f32[16,1,16,25,400]{4,2,3,1,0:T(8,128)}, u32[]{:S(2)}, u32[]{:S(2)}) async-start(f32[16,1,16,25,400]{4,2,3,1,0:T(8,128)} %stack.2), calls=%async_computation | async-start | bytes 26214400 | tf_op jit(solution)/shard_map/all_to_all | solution.py:15
  25.9 18.3 %copy.18 = f32[4,64,25,400]{3,2,1,0:T(8,128)} copy(f32[4,64,25,400]{3,1,2,0:T(8,128)} %param.6) | data formatting | bytes 20480000 | tf_op args[1]
  44.2 15.8 %reshape.59 = f32[4,64,10000,1]{2,1,0,3:T(8,128)} reshape(f32[4,64,25,400]{3,2,1,0:T(8,128)} %copy.18) | data formatting | bytes 20480000 | tf_op jit(solution)/shard_map/dot_general | solution.py:19
  60.0 261.4 %all-to-all-done = f32[16,1,16,25,400]{4,2,3,1,0:T(8,128)} async-done(((f32[16,1,16,25,400]{4,2,3,1,0:T(8,128)}), f32[16,1,16,25,400]{4,2,3,1,0:T(8,128)}, u32[]{:S(2)}, u32[]{:S(2)}) %all-to-all-start) | async-done | bytes 10240032 | tf_op jit(solution)/shard_map/all_to_all | solution.py:15
  321.4 21.4 %copy.17 = f32[16,1,16,25,400]{4,3,2,0,1:T(8,128)} copy(f32[16,1,16,25,400]{4,2,3,1,0:T(8,128)} %all-to-all-done) | data formatting | bytes 20480000 | tf_op jit(solution)/shard_map/all_to_all | solution.py:15
  342.8 15.8 %reshape.58 = f32[16,16,10000,1]{2,1,0,3:T(8,128)} reshape(f32[16,1,16,25,400]{4,3,2,0,1:T(8,128)} %copy.17) | data formatting | bytes 20480000 | tf_op jit(solution)/shard_map/dot_general | solution.py:19
  358.7 20.9 %fusion = f32[16,16,4,64]{3,1,2,0:T(8,128)} fusion(f32[4,64,10000,1]{2,1,0,3:T(8,128)} %reshape.59, f32[16,16,10000,1]{2,1,0,3:T(8,128)} %reshape.58), kind=kOutput, calls=%fused_computation | convolution fusion | flops 7864320000 | bytes 20742144 | tf_op jit(solution)/shard_map/dot_general | solution.py:19
  379.6 61.0 %reduce-scatter.2.cloned.1.call-done = f32[1,16,4,64]{3,1,2,0:T(8,128)} async-done(((f32[16,16,4,64]{3,1,2,0:T(8,128)}), f32[1,16,4,64]{3,1,2,0:T(8,128)}) %reduce-scatter.2.cloned.1.call-update) | async-done | bytes 16400 | tf_op jit(solution)/shard_map/reduce_scatter | solution.py:27
  440.5 0.9 copy.19
  441.4 0.7 reshape.62
  442.1 9.0 %all-to-all-start.1 = ((f32[16,1,256]{2,1,0:T(1,128)}), f32[16,1,256]{2,1,0:T(1,128)S(1)}, u32[]{:S(2)}, u32[]{:S(2)}) async-start(f32[16,1,256]{2,1,0:T(1,128)} %reshape.62), calls=%async_computation.2 | async-start | bytes 32768 | tf_op jit(solution)/shard_map/all_to_all | solution.py:29
  451.3 0.7 dynamic_slice.7
  451.9 8.2 %all-to-all-done.1 = f32[16,1,256]{2,1,0:T(1,128)S(1)} async-done(((f32[16,1,256]{2,1,0:T(1,128)}), f32[16,1,256]{2,1,0:T(1,128)S(1)}, u32[]{:S(2)}, u32[]{:S(2)}) %all-to-all-start.1) | async-done | bytes 16416 | tf_op jit(solution)/shard_map/all_to_all | solution.py:29
  460.1 0.5 broadcast.51
  460.6 0.6 reduce
  461.2 0.1 reshape.63
  461.5 0.7 reshape.64
  462.3 8.4 %all-to-all-start.2 = ((f32[16,1,256]{2,1,0:T(1,128)}), f32[16,1,256]{2,1,0:T(1,128)S(1)}, u32[]{:S(2)}, u32[]{:S(2)}) async-start(f32[16,1,256]{2,1,0:T(1,128)} %reshape.64), calls=%async_computation.3 | async-start | bytes 32768 | tf_op jit(solution)/shard_map/all_to_all | solution.py:28
  470.7 0.8 add_subtract_fusion
  471.4 5.1 %all-to-all-done.2 = f32[16,1,256]{2,1,0:T(1,128)S(1)} async-done(((f32[16,1,256]{2,1,0:T(1,128)}), f32[16,1,256]{2,1,0:T(1,128)S(1)}, u32[]{:S(2)}, u32[]{:S(2)}) %all-to-all-start.2) | async-done | bytes 16416 | tf_op jit(solution)/shard_map/all_to_all | solution.py:28
  476.5 0.6 reduce.1
  477.2 0.8 fusion.3
  478.1 0.6 copy.25
  (13 shorter events, 0.4 us)
Async XLA Ops:
  14.0 307.4 %all-to-all-start = ((f32[16,1,16,25,400]{4,2,3,1,0:T(8,128)}), f32[16,1,16,25,400]{4,2,3,1,0:T(8,128)}, u32[]{:S(2)}, u32[]{:S(2)}) async-start(f32[16,1,16,25,400]{4,2,3,1,0:T(8,128)} %stack.2), calls=%async_computation | async-start | bytes 26214400 | tf_op jit(solution)/shard_map/all_to_all | solution.py:15
  25.8 414.7 %reduce-scatter.2.cloned.1.call-start = ((), (), s32[]{:S(2)}) async-start(), calls=%async_computation.4 | async-start | bytes 557056 | tf_op jit(solution)/shard_map/reduce_scatter | solution.py:27
  358.7 92.5 %copy-start.2 = (f32[64]{0:T(128)S(1)}, f32[64]{0:T(128)}, u32[]{:S(2)}) copy-start(f32[64]{0:T(128)} %param.9) | copy-start | bytes 772
  358.7 92.6 %copy-start.1 = (f32[16]{0:T(128)S(1)}, f32[16]{0:T(128)}, u32[]{:S(2)}) copy-start(f32[16]{0:T(128)} %param.8) | copy-start | bytes 196
  358.7 118.6 %copy-start = (f32[1,16,4,64]{3,2,1,0:T(4,128)S(1)}, f32[1,16,4,64]{3,2,1,0:T(4,128)}, u32[]{:S(2)}) copy-start(f32[1,16,4,64]{3,2,1,0:T(4,128)} %param.7) | copy-start | bytes 49156
  442.1 18.0 %all-to-all-start.1 = ((f32[16,1,256]{2,1,0:T(1,128)}), f32[16,1,256]{2,1,0:T(1,128)S(1)}, u32[]{:S(2)}, u32[]{:S(2)}) async-start(f32[16,1,256]{2,1,0:T(1,128)} %reshape.62), calls=%async_computation.2 | async-start | bytes 32768 | tf_op jit(solution)/shard_map/all_to_all | solution.py:29
  462.3 14.3 %all-to-all-start.2 = ((f32[16,1,256]{2,1,0:T(1,128)}), f32[16,1,256]{2,1,0:T(1,128)S(1)}, u32[]{:S(2)}, u32[]{:S(2)}) async-start(f32[16,1,256]{2,1,0:T(1,128)} %reshape.64), calls=%async_computation.3 | async-start | bytes 32768 | tf_op jit(solution)/shard_map/all_to_all | solution.py:28
Sparse Core Ops, SparseCore 0:
  379.7 60.7 reduce-scatter.1
